TPU v7x, 32 devices: a whole 2x2x4 slice. The times are simulated.
32 devices in a mesh: sub: 8 (over y, x, core), front: 4 (over z).
Axes of the slice: x: 2, y: 2, z: 4, core: 2. Of those that a mesh axis runs over, the one named last changes fastest.
Arguments:
- front_inverse: bfloat16 [8, 8192, 2048], P('sub', 'front'), may hold values from -0.75 to 0.75
- coupling: bfloat16 [8, 8192, 2048], P('sub', 'front'), may hold values from -0.0234375 to 0.0234375
- free_modes: bfloat16 [8, 300, 8192], P('sub', None, 'front'), may hold values from -0.125 to 0.125
- dof_offset: int32 [8, 256], P('sub', 'front'), may hold values from 0 to 2047, as said below
- interface_id: int32 [8, 256], replicated, may hold values from 0 to 1023, as said below
Outputs:
- attachment: bfloat16 [8, 256, 8192], P('sub', None, 'front')
- flexibility: float32 [1024, 1024], P(('sub', 'front'))
Inputs may be any that keep to these rules, and one draw needn't show every extreme that they name: `dof_offset`: within one substructure and one front the 64 offsets are distinct, and 0 and 2047 occur among them. `interface_id`: every value occurs exactly twice in the whole array.
All inputs are finite; a program needn't handle non-finite values.
Results may differ from a plain program's by a relative error of at most 0.02.
Values may be sent and summed in bfloat16 or wider, within the bound.
No kernel may reach another device: no remote copies, remote signals or barrier semaphores. Data moves between devices by JAX's collectives and lax.ppermute only.
A program may use at most 128 MiB of HBM per device.

v0:
```python
import jax
import jax.numpy as jnp
from jax import lax
from jax.sharding import PartitionSpec as P


def shifted(value, axis, steps):
    count = lax.axis_size(axis)
    leading, last = (max(0, -steps), min(count, count - steps))
    return lax.ppermute(value, axis, [(source, source + steps) for source in range(leading, last)])


def contract_last(left, right):
    return lax.dot_general(
        left, right, (((1,), (1,)), ((), ())), preferred_element_type=jnp.float32
    )


def on_device(front_inverse, coupling, free_modes, dof_offset, interface_id):
    inverse_block = front_inverse[0]
    coupling_block = coupling[0]
    mode_block = free_modes[0]
    offsets = dof_offset[0]
    order = inverse_block.shape[0]
    columns_all = interface_id.shape[1]
    per_front = offsets.shape[0]
    fronts = lax.axis_size("front")
    front_pos = lax.axis_index("front")
    sub_pos = lax.axis_index("sub")
    column_ids = jnp.arange(columns_all, dtype=jnp.int32)
    local_ids = jnp.arange(per_front, dtype=jnp.int32)
    row_ids = jnp.arange(order, dtype=jnp.int32)
    column_pick = (column_ids[:, None] == front_pos * per_front + local_ids[None, :]).astype(
        jnp.float32
    )
    row_pick = (offsets[:, None] == row_ids[None, :]).astype(jnp.float32)
    forces = jnp.dot(column_pick, row_pick, precision=lax.Precision.HIGHEST)
    groups = 1
    width = columns_all // groups
    force_groups = forces.reshape(groups, width, order)
    moments = groups + fronts - 1

    def forward(moment, carry):
        solved, outgoing = carry
        incoming = shifted(outgoing, "front", 1)
        panel = moment - front_pos
        valid = (panel >= 0) & (panel < groups)
        clipped = jnp.clip(panel, 0, groups - 1)

        def forward_active(unused):
            load = lax.dynamic_index_in_dim(force_groups, clipped, 0, keepdims=False)
            reduced = (load - contract_last(incoming, coupling_block)).astype(jnp.bfloat16)
            return contract_last(reduced, inverse_block).astype(jnp.bfloat16)

        def forward_waiting(unused):
            return outgoing

        result = lax.cond(valid, forward_active, forward_waiting, 0)
        solved = lax.dynamic_update_index_in_dim(solved, result, clipped, 0)
        return (solved, result)

    forward_start = (
        jnp.zeros((groups, width, order), jnp.bfloat16),
        jnp.zeros((width, order), jnp.bfloat16),
    )
    solved, forward_last = lax.fori_loop(0, moments, forward, forward_start)

    def backward(moment, carry):
        moved, outgoing = carry
        incoming = shifted(outgoing, "front", -1)
        panel = moment - (fronts - 1 - front_pos)
        valid = (panel >= 0) & (panel < groups)
        clipped = jnp.clip(panel, 0, groups - 1)

        def backward_active(unused):
            upper = lax.dynamic_index_in_dim(solved, clipped, 0, keepdims=False).astype(jnp.float32)
            reduced = (upper - incoming.astype(jnp.float32)).astype(jnp.bfloat16)
            displaced = jnp.dot(reduced, inverse_block, preferred_element_type=jnp.float32)
            handed = jnp.dot(
                displaced.astype(jnp.bfloat16), coupling_block, preferred_element_type=jnp.float32
            )
            return (displaced, handed.astype(jnp.bfloat16))

        def backward_waiting(unused):
            return (lax.dynamic_index_in_dim(moved, clipped, 0, keepdims=False), outgoing)

        displaced, handed = lax.cond(valid, backward_active, backward_waiting, 0)
        moved = lax.dynamic_update_index_in_dim(moved, displaced, clipped, 0)
        return (moved, handed)

    backward_start = (
        jnp.zeros((groups, width, order), jnp.float32),
        jnp.zeros((width, order), jnp.bfloat16),
    )
    moved, backward_last = lax.fori_loop(0, moments, backward, backward_start)
    displacement = moved.reshape(columns_all, order)
    modal = lax.psum(
        contract_last(displacement.astype(jnp.bfloat16), mode_block).astype(jnp.bfloat16), "front"
    )
    deflated = displacement - jnp.dot(modal, mode_block, preferred_element_type=jnp.float32)
    own_rows = jnp.take(deflated, offsets, axis=1).T
    total_ids = interface_id.shape[0] * columns_all // 2
    dual_ids = jnp.arange(total_ids, dtype=jnp.int32)
    owners = lax.axis_size("sub") * fronts
    share = total_ids // owners
    gathered = lax.all_gather(
        own_rows.astype(jnp.bfloat16), ("sub", "front"), axis=0, tiled=True
    ).astype(own_rows.dtype)
    subs_all = interface_id.shape[0]
    flat_labels = interface_id.reshape(-1)
    owner_pos = sub_pos * fronts + front_pos
    targets = owner_pos * share + jnp.arange(share, dtype=jnp.int32)
    row_select = (targets[:, None] == flat_labels[None, :]).astype(jnp.float32)
    reduced = jnp.einsum(
        "asc,scd->asd",
        row_select.reshape(share, subs_all, columns_all),
        gathered.reshape(subs_all, columns_all, columns_all),
        precision=lax.Precision.HIGHEST,
    )
    column_place = (flat_labels[:, None] == dual_ids[None, :]).astype(jnp.float32)
    flexibility = jnp.dot(
        reduced.reshape(share, subs_all * columns_all),
        column_place,
        precision=lax.Precision.HIGHEST,
    )
    return (deflated.astype(jnp.bfloat16)[None], flexibility)


def solution(mesh):
    return jax.shard_map(
        on_device,
        mesh=mesh,
        in_specs=(
            P("sub", "front", None),
            P("sub", "front", None),
            P("sub", None, "front"),
            P("sub", "front"),
            P(),
        ),
        out_specs=(P("sub", None, "front"), P(("sub", "front"), None)),
        check_vma=False,
    )
```

profile of v0, /device:TPU:0, one launch (start us, length us, event | category | flops | bytes accessed | tf_op | source)
XLA Modules:
  0.0 390.6 jit_solution(3004368580467127556)
XLA Ops:
  7.2 0.0 copy-start
  7.2 0.0 all-reduce.2.cloned.1.call-start
  7.3 2.6 convolution_bitcast_fusion
  9.8 0.1 broadcast.48.clone
  9.9 126.6 %while.35 = (s32[]{:T(128)}, bf16[1,256,2048]{2,1,0:T(8,128)(2,1)}, bf16[256,2048]{1,0:T(8,128)(2,1)S(1)}, s32[]{:T(128)}, f32[1,256,2048]{2,1,0:T(8,128)}, /*in...) while((s32[]{:T(128)}, bf16[1,256,2048]{2,1,0:T(8,128)(2,1)}, ...), condition=%wide.region_3.4_spmd, body=%wide.region_0.3_spmd.sunk | while | flops 4296540160 | bytes 33554672 | solution.py:66
  10.0 0.1 copy.23
  10.1 5.0 %collective-permute-start = (bf16[256,2048]{1,0:T(8,128)(2,1)S(1)}, bf16[256,2048]{1,0:T(8,128)(2,1)S(1)}, u32[]{:S(2)}, u32[]{:S(2)}) collective-permute-start(bf16[256,2048]{1,0:T(8,128)(2,1)S(1)} %copy.23), channel_id=1, source_target_pairs={{0,1},{1,2},{2,3},{4,5},{5,6},{6,7},{8,9},{9,10},{10,11},{12,13},{... | collective-permute-start | bytes 3145736 | tf_op jit(solution)/shard_map/while/body/eval_jaxpr/ppermute | solution.py:10
  15.1 22.3 %collective-permute-done = bf16[256,2048]{1,0:T(8,128)(2,1)S(1)} collective-permute-done((bf16[256,2048]{1,0:T(8,128)(2,1)S(1)}, bf16[256,2048]{1,0:T(8,128)(2,1)S(1)}, u32[]{:S(2)}, u32[]{:S(2)}) %collective-permute-start) | collective-permute-done | bytes 1048608 | tf_op jit(solution)/shard_map/while/body/eval_jaxpr/ppermute | solution.py:10
  37.4 10.9 %conditional.4 = (bf16[256,2048]{1,0:T(8,128)(2,1)S(1)}) conditional(s32[]{:T(128)} %convert_element_type.98, bf16[256,2048]{1,0:T(8,128)(2,1)S(1)} %copy.23, (f32[1,256,2048]{2,1,0:T(8,128)}, bf16[256,2048]{1,0:T(8,128)(2,1)S(1)}, bf16[2048,2048]{1,0:T(8,128)(2,1)}, bf16[2048,2048]{1,0:T(8,128)(2,1)}) %tuple.101), branch_computations={%region_1.1_spmd, %region_2.2_spmd} | conditional | flops 4296540160 | bytes 20971528 | solution.py:58
  37.4 10.9 %convolution_convert_fusion = bf16[256,2048]{1,0:T(8,128)(2,1)S(1)} fusion(bf16[2048,2048]{1,0:T(8,128)(2,1)} %get-tuple-element.340, bf16[256,2048]{1,0:T(8,128)(2,1)S(1)} %get-tuple-element.338, bf16[2048,2048]{1,0:T(8,128)(2,1)} %get-tuple-element.339, f32[1,256,2048]{2,1,0:T(8,128)} %get-tuple-element.337), kind=kOutput, calls=%fused_computation.3 | convolution fusion | flops 4296540160 | bytes 20971520 | tf_op jit(solution)/shard_map/while/body/eval_jaxpr/cond/branch_1_fun/dot_general | solution.py:14
  48.4 0.0 copy-start.1
  48.4 0.1 copy.26
  48.5 0.9 copy-done.1
  49.3 0.1 copy.23
  49.4 1.4 collective-permute-start
  50.8 21.8 %collective-permute-done = bf16[256,2048]{1,0:T(8,128)(2,1)S(1)} collective-permute-done((bf16[256,2048]{1,0:T(8,128)(2,1)S(1)}, bf16[256,2048]{1,0:T(8,128)(2,1)S(1)}, u32[]{:S(2)}, u32[]{:S(2)}) %collective-permute-start) | collective-permute-done | bytes 1048608 | tf_op jit(solution)/shard_map/while/body/eval_jaxpr/ppermute | solution.py:10
  72.6 0.1 copy.26
  72.7 0.9 copy-done.1
  73.5 0.1 copy.23
  73.6 15.4 %collective-permute-start = (bf16[256,2048]{1,0:T(8,128)(2,1)S(1)}, bf16[256,2048]{1,0:T(8,128)(2,1)S(1)}, u32[]{:S(2)}, u32[]{:S(2)}) collective-permute-start(bf16[256,2048]{1,0:T(8,128)(2,1)S(1)} %copy.23), channel_id=1, source_target_pairs={{0,1},{1,2},{2,3},{4,5},{5,6},{6,7},{8,9},{9,10},{10,11},{12,13},{... | collective-permute-start | bytes 3145736 | tf_op jit(solution)/shard_map/while/body/eval_jaxpr/ppermute | solution.py:10
  89.1 20.9 %collective-permute-done = bf16[256,2048]{1,0:T(8,128)(2,1)S(1)} collective-permute-done((bf16[256,2048]{1,0:T(8,128)(2,1)S(1)}, bf16[256,2048]{1,0:T(8,128)(2,1)S(1)}, u32[]{:S(2)}, u32[]{:S(2)}) %collective-permute-start) | collective-permute-done | bytes 1048608 | tf_op jit(solution)/shard_map/while/body/eval_jaxpr/ppermute | solution.py:10
  110.0 0.1 copy.26
  110.1 0.9 copy-done.1
  110.9 0.1 copy.23
  111.0 4.5 %collective-permute-start = (bf16[256,2048]{1,0:T(8,128)(2,1)S(1)}, bf16[256,2048]{1,0:T(8,128)(2,1)S(1)}, u32[]{:S(2)}, u32[]{:S(2)}) collective-permute-start(bf16[256,2048]{1,0:T(8,128)(2,1)S(1)} %copy.23), channel_id=1, source_target_pairs={{0,1},{1,2},{2,3},{4,5},{5,6},{6,7},{8,9},{9,10},{10,11},{12,13},{... | collective-permute-start | bytes 3145736 | tf_op jit(solution)/shard_map/while/body/eval_jaxpr/ppermute | solution.py:10
  115.5 20.0 %collective-permute-done = bf16[256,2048]{1,0:T(8,128)(2,1)S(1)} collective-permute-done((bf16[256,2048]{1,0:T(8,128)(2,1)S(1)}, bf16[256,2048]{1,0:T(8,128)(2,1)S(1)}, u32[]{:S(2)}, u32[]{:S(2)}) %collective-permute-start) | collective-permute-done | bytes 1048608 | tf_op jit(solution)/shard_map/while/body/eval_jaxpr/ppermute | solution.py:10
  135.5 0.1 copy.26
  135.6 0.9 copy-done.1
  136.5 1.6 broadcast_in_dim.49
  138.1 0.1 broadcast.48
  138.2 0.0 copy-done.2
  138.2 144.6 %while.36 = (s32[]{:T(128)}, f32[1,256,2048]{2,1,0:T(8,128)}, bf16[256,2048]{1,0:T(8,128)(2,1)S(1)}, s32[]{:T(128)}, bf16[1,256,2048]{2,1,0:T(8,128)(2,1)S(1)}, ...) while((s32[]{:T(128)}, f32[1,256,2048]{2,1,0:T(8,128)}, ...), condition=%wide.region_7.8_spmd, body=%wide.region_4.7_spmd.sunk | while | flops 4298113024 | bytes 70254888 | solution.py:95
  138.2 1.3 collective-permute-start.1
  139.5 32.5 %collective-permute-done.1 = bf16[256,2048]{1,0:T(8,128)(2,1)} collective-permute-done((bf16[256,2048]{1,0:T(8,128)(2,1)S(1)}, bf16[256,2048]{1,0:T(8,128)(2,1)}, u32[]{:S(2)}, u32[]{:S(2)}) %collective-permute-start.1) | collective-permute-done | bytes 1048608 | tf_op jit(solution)/shard_map/while/body/eval_jaxpr/ppermute | solution.py:10
  172.1 1.3 collective-permute-start.1
  173.4 22.9 %collective-permute-done.1 = bf16[256,2048]{1,0:T(8,128)(2,1)} collective-permute-done((bf16[256,2048]{1,0:T(8,128)(2,1)S(1)}, bf16[256,2048]{1,0:T(8,128)(2,1)}, u32[]{:S(2)}, u32[]{:S(2)}) %collective-permute-start.1) | collective-permute-done | bytes 1048608 | tf_op jit(solution)/shard_map/while/body/eval_jaxpr/ppermute | solution.py:10
  196.3 1.3 collective-permute-start.1
  197.5 31.3 %collective-permute-done.1 = bf16[256,2048]{1,0:T(8,128)(2,1)} collective-permute-done((bf16[256,2048]{1,0:T(8,128)(2,1)S(1)}, bf16[256,2048]{1,0:T(8,128)(2,1)}, u32[]{:S(2)}, u32[]{:S(2)}) %collective-permute-start.1) | collective-permute-done | bytes 1048608 | tf_op jit(solution)/shard_map/while/body/eval_jaxpr/ppermute | solution.py:10
  228.8 1.3 collective-permute-start.1
  230.1 44.1 %collective-permute-done.1 = bf16[256,2048]{1,0:T(8,128)(2,1)} collective-permute-done((bf16[256,2048]{1,0:T(8,128)(2,1)S(1)}, bf16[256,2048]{1,0:T(8,128)(2,1)}, u32[]{:S(2)}, u32[]{:S(2)}) %collective-permute-start.1) | collective-permute-done | bytes 1048608 | tf_op jit(solution)/shard_map/while/body/eval_jaxpr/ppermute | solution.py:10
  274.2 8.5 %conditional.5 = ((bf16[256,2048]{1,0:T(8,128)(2,1)S(1)}, f32[1,256,2048]{2,1,0:T(8,128)})) conditional(s32[]{:T(128)} %convert_element_type.99, (bf16[256,2048]{1,0:T(8,128)(2,1)S(1)}, f32[1,256,2048]{2,1,0:T(8,128)}) %tuple.103, (bf16[1,256,2048]{2,1,0:T(8,128)(2,1)S(1)}, bf16[256,2048]{1,0:T(8,128)(2,1)}, bf16[2048,2048]{1,0:T(8,128)(2,1)}, ...), branch_computations={%region_5.5_spmd, %region_6.6_spmd} | conditional | flops 4298113024 | bytes 66060368 | solution.py:87
  274.2 6.2 %fusion.2 = f32[256,2048]{1,0:T(8,128)S(1)} fusion(bf16[2048,2048]{1,0:T(8,128)(2,1)} %get-tuple-element.350, bf16[256,2048]{1,0:T(8,128)(2,1)} %get-tuple-element.349, bf16[1,256,2048]{2,1,0:T(8,128)(2,1)S(1)} %get-tuple-element.348), kind=kOutput, calls=%fused_computation.7 | convolution fusion | flops 2149580800 | bytes 12582912 | tf_op jit(solution)/shard_map/while/body/eval_jaxpr/cond/branch_1_fun/dot_general | solution.py:78
  280.4 0.0 copy-start.3
  280.4 0.0 copy-done.7
  280.4 2.3 convolution_convert_fusion.1
  282.8 0.0 copy-done.3
  282.8 0.0 copy-start.6
  282.8 0.0 copy-start.4
  282.8 0.0 copy-done
  282.8 3.1 fusion.11
  286.0 0.0 all-reduce.2.cloned.1.call-update
  286.0 0.2 all-gather.2.cloned.1.call-start
  286.2 0.0 copy-done.6
  286.3 33.1 %all-reduce.2.cloned.1.call-done = bf16[256,300]{1,0:T(8,128)(2,1)} async-done(((bf16[256,300]{1,0:T(8,128)(2,1)}), bf16[256,300]{1,0:T(8,128)(2,1)}) %all-reduce.2.cloned.1.call-update) | async-done | bytes 153616 | tf_op jit(solution)/shard_map/psum | solution.py:97
  319.3 0.0 copy-done.4
  319.4 2.6 convolution_subtract_fusion.1
  322.0 1.5 copy.8
  323.5 0.7 gather_fusion
  324.2 0.7 select_convert_fusion
  324.9 0.0 all-gather.2.cloned.1.call-update
  324.9 0.0 copy-done.5
  324.9 53.6 %all-gather.2.cloned.1.call-done = bf16[2048,256]{1,0:T(8,128)(2,1)} async-done(((bf16[64,256]{1,0:T(8,128)(2,1)}), bf16[2048,256]{1,0:T(8,128)(2,1)}) %all-gather.2.cloned.1.call-update) | async-done | bytes 1048592 | tf_op jit(solution)/shard_map/all_gather | solution.py:106
  378.5 1.5 convolution_bitcast_fusion.1
  380.1 3.8 fusion.6
  (20 shorter events, 0.1 us)
Async XLA Ops:
  7.2 275.7 %copy-start = (bf16[1,300,2048]{2,1,0:T(8,128)(2,1)S(1)}, bf16[1,300,2048]{2,1,0:T(8,128)(2,1)}, u32[]{:S(2)}) copy-start(bf16[1,300,2048]{2,1,0:T(8,128)(2,1)} %param.15) | copy-start | bytes 3686404
  7.2 312.2 %all-reduce.2.cloned.1.call-start = ((), (), s32[]{:S(2)}) async-start(), calls=%async_computation | async-start | bytes 393216 | tf_op jit(solution)/shard_map/psum | solution.py:97
  10.1 27.4 %collective-permute-start = (bf16[256,2048]{1,0:T(8,128)(2,1)S(1)}, bf16[256,2048]{1,0:T(8,128)(2,1)S(1)}, u32[]{:S(2)}, u32[]{:S(2)}) collective-permute-start(bf16[256,2048]{1,0:T(8,128)(2,1)S(1)} %copy.23), channel_id=1, source_target_pairs={{0,1},{1,2},{2,3},{4,5},{5,6},{6,7},{8,9},{9,10},{10,11},{12,13},{... | collective-permute-start | bytes 3145736 | tf_op jit(solution)/shard_map/while/body/eval_jaxpr/ppermute | solution.py:10
  48.4 1.0 copy-start.1
  49.4 23.1 %collective-permute-start = (bf16[256,2048]{1,0:T(8,128)(2,1)S(1)}, bf16[256,2048]{1,0:T(8,128)(2,1)S(1)}, u32[]{:S(2)}, u32[]{:S(2)}) collective-permute-start(bf16[256,2048]{1,0:T(8,128)(2,1)S(1)} %copy.23), channel_id=1, source_target_pairs={{0,1},{1,2},{2,3},{4,5},{5,6},{6,7},{8,9},{9,10},{10,11},{12,13},{... | collective-permute-start | bytes 3145736 | tf_op jit(solution)/shard_map/while/body/eval_jaxpr/ppermute | solution.py:10
  72.6 1.0 copy-start.1
  73.6 36.3 %collective-permute-start = (bf16[256,2048]{1,0:T(8,128)(2,1)S(1)}, bf16[256,2048]{1,0:T(8,128)(2,1)S(1)}, u32[]{:S(2)}, u32[]{:S(2)}) collective-permute-start(bf16[256,2048]{1,0:T(8,128)(2,1)S(1)} %copy.23), channel_id=1, source_target_pairs={{0,1},{1,2},{2,3},{4,5},{5,6},{6,7},{8,9},{9,10},{10,11},{12,13},{... | collective-permute-start | bytes 3145736 | tf_op jit(solution)/shard_map/while/body/eval_jaxpr/ppermute | solution.py:10
  110.0 1.0 copy-start.1
  111.0 24.5 %collective-permute-start = (bf16[256,2048]{1,0:T(8,128)(2,1)S(1)}, bf16[256,2048]{1,0:T(8,128)(2,1)S(1)}, u32[]{:S(2)}, u32[]{:S(2)}) collective-permute-start(bf16[256,2048]{1,0:T(8,128)(2,1)S(1)} %copy.23), channel_id=1, source_target_pairs={{0,1},{1,2},{2,3},{4,5},{5,6},{6,7},{8,9},{9,10},{10,11},{12,13},{... | collective-permute-start | bytes 3145736 | tf_op jit(solution)/shard_map/while/body/eval_jaxpr/ppermute | solution.py:10
  135.5 1.0 copy-start.1
  136.5 1.7 copy-start.2
  138.2 33.8 %collective-permute-start.1 = (bf16[256,2048]{1,0:T(8,128)(2,1)S(1)}, bf16[256,2048]{1,0:T(8,128)(2,1)}, u32[]{:S(2)}, u32[]{:S(2)}) collective-permute-start(bf16[256,2048]{1,0:T(8,128)(2,1)S(1)} %get-tuple-element.526), channel_id=1, source_target_pairs={{1,0},{2,1},{3,2},{5,4},{6,5},{7,6},{9,8},{10,9},{11,10},{13,12},{... | collective-permute-start | bytes 3145736 | tf_op jit(solution)/shard_map/while/body/eval_jaxpr/ppermute | solution.py:10
  172.1 24.2 %collective-permute-start.1 = (bf16[256,2048]{1,0:T(8,128)(2,1)S(1)}, bf16[256,2048]{1,0:T(8,128)(2,1)}, u32[]{:S(2)}, u32[]{:S(2)}) collective-permute-start(bf16[256,2048]{1,0:T(8,128)(2,1)S(1)} %get-tuple-element.526), channel_id=1, source_target_pairs={{1,0},{2,1},{3,2},{5,4},{6,5},{7,6},{9,8},{10,9},{11,10},{13,12},{... | collective-permute-start | bytes 3145736 | tf_op jit(solution)/shard_map/while/body/eval_jaxpr/ppermute | solution.py:10
  196.3 32.6 %collective-permute-start.1 = (bf16[256,2048]{1,0:T(8,128)(2,1)S(1)}, bf16[256,2048]{1,0:T(8,128)(2,1)}, u32[]{:S(2)}, u32[]{:S(2)}) collective-permute-start(bf16[256,2048]{1,0:T(8,128)(2,1)S(1)} %get-tuple-element.526), channel_id=1, source_target_pairs={{1,0},{2,1},{3,2},{5,4},{6,5},{7,6},{9,8},{10,9},{11,10},{13,12},{... | collective-permute-start | bytes 3145736 | tf_op jit(solution)/shard_map/while/body/eval_jaxpr/ppermute | solution.py:10
  228.8 45.4 %collective-permute-start.1 = (bf16[256,2048]{1,0:T(8,128)(2,1)S(1)}, bf16[256,2048]{1,0:T(8,128)(2,1)}, u32[]{:S(2)}, u32[]{:S(2)}) collective-permute-start(bf16[256,2048]{1,0:T(8,128)(2,1)S(1)} %get-tuple-element.526), channel_id=1, source_target_pairs={{1,0},{2,1},{3,2},{5,4},{6,5},{7,6},{9,8},{10,9},{11,10},{13,12},{... | collective-permute-start | bytes 3145736 | tf_op jit(solution)/shard_map/while/body/eval_jaxpr/ppermute | solution.py:10
  274.2 6.2 %copy-start.7 = (bf16[2048,2048]{1,0:T(8,128)(2,1)S(1)}, bf16[2048,2048]{1,0:T(8,128)(2,1)}, u32[]{:S(2)}) copy-start(bf16[2048,2048]{1,0:T(8,128)(2,1)} %get-tuple-element.351) | copy-start | bytes 25165828 | tf_op jit(solution)/shard_map/while/body/eval_jaxpr/cond
  280.4 2.4 copy-start.3
  282.8 3.4 copy-start.6
  282.8 36.5 %copy-start.4 = (f32[1,256,2048]{2,1,0:T(8,128)S(1)}, f32[1,256,2048]{2,1,0:T(8,128)}, u32[]{:S(2)}) copy-start(f32[1,256,2048]{2,1,0:T(8,128)} %get-tuple-element.367) | copy-start | bytes 6291460
  286.0 92.5 %all-gather.2.cloned.1.call-start = ((), (), s32[]{:S(2)}) async-start(), calls=%async_computation.1 | async-start | bytes 1081344 | tf_op jit(solution)/shard_map/all_gather | solution.py:106
  322.0 2.9 copy-start.5
Sparse Core Ops, SparseCore 0:
  286.1 33.1 all-reduce.1
  325.0 53.4 all-gather.1
where the time goes:
time: 391 us
  waiting for transfers between devices  302 us (77%)
  matrix products  33 us (8%)
  starting transfers between devices  31.6 us (8%)
  between operations  14.2 us (4%)
  local copies, waits for them, and re-layouts  8.29 us (2%)
    ppermute x8, waiting for transfers between devices, shifted(): lax.ppermute(value, axis, [(source, source + steps) for source in range(l...  216 us
    all_gather x1, waiting for transfers between devices, on_device(): lax.all_gather(own_rows.astype(jnp.bfloat16), ('sub', 'front'), axis=0, t...  53.6 us
    psum x1, waiting for transfers between devices, on_device(): lax.psum(contract_last(displacement.astype(jnp.bfloat16), mode_block).ast...  33.1 us
    ppermute x8, starting transfers between devices, shifted(): lax.ppermute(value, axis, [(source, source + steps) for source in range(l...  31.4 us
    dot_general x2, matrix products, contract_last(): lax.dot_general(left, right, (((1,), (1,)), ((), ())), preferred_element_...  14.1 us
  transfers between devices with their start and end apart: 10, of which 10 were waited for; matrix products, arithmetic and copies ran while one was open for 0% of the time, Pallas kernels for 0%

commit v1 on v0

--- a/solution.py
+++ b/solution.py
@@ -2,6 +2,18 @@
 import jax.numpy as jnp
 from jax import lax
 from jax.sharding import PartitionSpec as P
+
+
+def collect(x, axis, dim):
+    ways, here, lap = (lax.axis_size(axis), lax.axis_index(axis), x.shape[dim])
+    line, have = (x, 1)
+    while have < ways:
+        line = jnp.concatenate(
+            [line, lax.ppermute(line, axis, [(d, (d - have) % ways) for d in range(ways)])],
+            axis=dim,
+        )
+        have = 2 * have
+    return jnp.roll(line, here * lap, axis=dim)
 
 
 def shifted(value, axis, steps):
@@ -103,9 +115,7 @@
     dual_ids = jnp.arange(total_ids, dtype=jnp.int32)
     owners = lax.axis_size("sub") * fronts
     share = total_ids // owners
-    gathered = lax.all_gather(
-        own_rows.astype(jnp.bfloat16), ("sub", "front"), axis=0, tiled=True
-    ).astype(own_rows.dtype)
+    gathered = collect(own_rows.astype(jnp.bfloat16), ("sub", "front"), 0).astype(own_rows.dtype)
     subs_all = interface_id.shape[0]
     flat_labels = interface_id.reshape(-1)
     owner_pos = sub_pos * fronts + front_pos

time: 391 us -> 378 us (0.967)
  waiting for transfers between devices: 302 us -> 277 us
  local copies, waits for them, and re-layouts: 8.29 us -> 17.7 us
  starting transfers between devices: 31.6 us -> 36.2 us
    all_gather x1 -> x0, waiting for transfers between devices: 53.6 us -> none  [on_device(): lax.all_gather(own_rows.astype(jnp.bfloat16), ('sub', 'front'), axis=0, t...]
    ppermute x0 -> x5, waiting for transfers between devices: none -> 27.8 us  [collect(): lax.ppermute(line, axis, [(d, (d - have) % ways) for d in range(ways)])]
    unnamed x11 -> x21, local copies, waits for them, and re-layouts: 0.03 us -> 6.57 us
    ppermute x0 -> x5, starting transfers between devices: none -> 4.77 us  [collect(): lax.ppermute(line, axis, [(d, (d - have) % ways) for d in range(ways)])]
  transfers between devices with their start and end apart: 10 -> 14, of which waited for: 10 -> 14; matrix products, arithmetic and copies ran while one was open for 0% -> 1% of each run, Pallas kernels for 0% -> 0%
where the time goes in v1:
time: 378 us; the launch traced here: 377 us
  waiting for transfers between devices  277 us (73%)
  starting transfers between devices  36.2 us (10%)
  matrix products  31.8 us (8%)
  local copies, waits for them, and re-layouts  17.7 us (5%)
  between operations  14.2 us (4%)
    ppermute x8, waiting for transfers between devices, shifted(): lax.ppermute(value, axis, [(source, source + steps) for source in range(l...  216 us
    psum x1, waiting for transfers between devices, on_device(): lax.psum(contract_last(displacement.astype(jnp.bfloat16), mode_block).ast...  33.3 us
    ppermute x8, starting transfers between devices, shifted(): lax.ppermute(value, axis, [(source, source + steps) for source in range(l...  31.4 us
    ppermute x5, waiting for transfers between devices, collect(): lax.ppermute(line, axis, [(d, (d - have) % ways) for d in range(ways)])  27.8 us
    dot_general x2, matrix products, contract_last(): lax.dot_general(left, right, (((1,), (1,)), ((), ())), preferred_element_...  14.1 us
  transfers between devices with their start and end apart: 14, of which 14 were waited for; matrix products, arithmetic and copies ran while one was open for 1% of the time, Pallas kernels for 0%

profile of v1, /device:TPU:0, one launch (start us, length us, event | category | flops | bytes accessed | tf_op | source)
XLA Modules:
  0.0 377.2 jit_solution(18032869375030888668)
XLA Ops:
  7.3 2.6 convolution_bitcast_fusion
  9.8 0.1 broadcast.49.clone
  9.9 126.6 %while.35 = (s32[]{:T(128)}, bf16[1,256,2048]{2,1,0:T(8,128)(2,1)}, bf16[256,2048]{1,0:T(8,128)(2,1)S(1)}, s32[]{:T(128)}, f32[1,256,2048]{2,1,0:T(8,128)}, /*in...) while((s32[]{:T(128)}, bf16[1,256,2048]{2,1,0:T(8,128)(2,1)}, ...), condition=%wide.region_3.4_spmd, body=%wide.region_0.3_spmd.sunk | while | flops 4296540160 | bytes 33554672 | solution.py:78
  9.9 0.1 copy.23
  10.1 5.0 %collective-permute-start = (bf16[256,2048]{1,0:T(8,128)(2,1)S(1)}, bf16[256,2048]{1,0:T(8,128)(2,1)S(1)}, u32[]{:S(2)}, u32[]{:S(2)}) collective-permute-start(bf16[256,2048]{1,0:T(8,128)(2,1)S(1)} %copy.23), channel_id=1, source_target_pairs={{0,1},{1,2},{2,3},{4,5},{5,6},{6,7},{8,9},{9,10},{10,11},{12,13},{... | collective-permute-start | bytes 3145736 | tf_op jit(solution)/shard_map/while/body/eval_jaxpr/ppermute | solution.py:22
  15.1 22.3 %collective-permute-done = bf16[256,2048]{1,0:T(8,128)(2,1)S(1)} collective-permute-done((bf16[256,2048]{1,0:T(8,128)(2,1)S(1)}, bf16[256,2048]{1,0:T(8,128)(2,1)S(1)}, u32[]{:S(2)}, u32[]{:S(2)}) %collective-permute-start) | collective-permute-done | bytes 1048608 | tf_op jit(solution)/shard_map/while/body/eval_jaxpr/ppermute | solution.py:22
  37.4 10.9 %conditional.4 = (bf16[256,2048]{1,0:T(8,128)(2,1)S(1)}) conditional(s32[]{:T(128)} %convert_element_type.98, bf16[256,2048]{1,0:T(8,128)(2,1)S(1)} %copy.23, (f32[1,256,2048]{2,1,0:T(8,128)}, bf16[256,2048]{1,0:T(8,128)(2,1)S(1)}, bf16[2048,2048]{1,0:T(8,128)(2,1)}, bf16[2048,2048]{1,0:T(8,128)(2,1)}) %tuple.106), branch_computations={%region_1.1_spmd, %region_2.2_spmd} | conditional | flops 4296540160 | bytes 20971528 | solution.py:70
  37.4 10.9 %convolution_convert_fusion = bf16[256,2048]{1,0:T(8,128)(2,1)S(1)} fusion(bf16[2048,2048]{1,0:T(8,128)(2,1)} %get-tuple-element.340, bf16[256,2048]{1,0:T(8,128)(2,1)S(1)} %get-tuple-element.338, bf16[2048,2048]{1,0:T(8,128)(2,1)} %get-tuple-element.339, f32[1,256,2048]{2,1,0:T(8,128)} %get-tuple-element.337), kind=kOutput, calls=%fused_computation.3 | convolution fusion | flops 4296540160 | bytes 20971520 | tf_op jit(solution)/shard_map/while/body/eval_jaxpr/cond/branch_1_fun/dot_general | solution.py:26
  48.4 0.1 copy.26
  48.5 0.9 copy-done.1
  49.4 1.4 collective-permute-start
  50.8 21.8 %collective-permute-done = bf16[256,2048]{1,0:T(8,128)(2,1)S(1)} collective-permute-done((bf16[256,2048]{1,0:T(8,128)(2,1)S(1)}, bf16[256,2048]{1,0:T(8,128)(2,1)S(1)}, u32[]{:S(2)}, u32[]{:S(2)}) %collective-permute-start) | collective-permute-done | bytes 1048608 | tf_op jit(solution)/shard_map/while/body/eval_jaxpr/ppermute | solution.py:22
  72.6 0.1 copy.26
  72.7 0.9 copy-done.1
  73.6 15.4 %collective-permute-start = (bf16[256,2048]{1,0:T(8,128)(2,1)S(1)}, bf16[256,2048]{1,0:T(8,128)(2,1)S(1)}, u32[]{:S(2)}, u32[]{:S(2)}) collective-permute-start(bf16[256,2048]{1,0:T(8,128)(2,1)S(1)} %copy.23), channel_id=1, source_target_pairs={{0,1},{1,2},{2,3},{4,5},{5,6},{6,7},{8,9},{9,10},{10,11},{12,13},{... | collective-permute-start | bytes 3145736 | tf_op jit(solution)/shard_map/while/body/eval_jaxpr/ppermute | solution.py:22
  89.1 20.9 %collective-permute-done = bf16[256,2048]{1,0:T(8,128)(2,1)S(1)} collective-permute-done((bf16[256,2048]{1,0:T(8,128)(2,1)S(1)}, bf16[256,2048]{1,0:T(8,128)(2,1)S(1)}, u32[]{:S(2)}, u32[]{:S(2)}) %collective-permute-start) | collective-permute-done | bytes 1048608 | tf_op jit(solution)/shard_map/while/body/eval_jaxpr/ppermute | solution.py:22
  110.1 0.9 copy-done.1
  111.0 4.5 %collective-permute-start = (bf16[256,2048]{1,0:T(8,128)(2,1)S(1)}, bf16[256,2048]{1,0:T(8,128)(2,1)S(1)}, u32[]{:S(2)}, u32[]{:S(2)}) collective-permute-start(bf16[256,2048]{1,0:T(8,128)(2,1)S(1)} %copy.23), channel_id=1, source_target_pairs={{0,1},{1,2},{2,3},{4,5},{5,6},{6,7},{8,9},{9,10},{10,11},{12,13},{... | collective-permute-start | bytes 3145736 | tf_op jit(solution)/shard_map/while/body/eval_jaxpr/ppermute | solution.py:22
  115.5 20.0 %collective-permute-done = bf16[256,2048]{1,0:T(8,128)(2,1)S(1)} collective-permute-done((bf16[256,2048]{1,0:T(8,128)(2,1)S(1)}, bf16[256,2048]{1,0:T(8,128)(2,1)S(1)}, u32[]{:S(2)}, u32[]{:S(2)}) %collective-permute-start) | collective-permute-done | bytes 1048608 | tf_op jit(solution)/shard_map/while/body/eval_jaxpr/ppermute | solution.py:22
  135.6 0.9 copy-done.1
  136.5 1.6 broadcast_in_dim.49
  138.1 0.1 broadcast.49
  138.2 144.6 %while.36 = (s32[]{:T(128)}, f32[1,256,2048]{2,1,0:T(8,128)}, bf16[256,2048]{1,0:T(8,128)(2,1)S(1)}, s32[]{:T(128)}, bf16[1,256,2048]{2,1,0:T(8,128)(2,1)S(1)}, ...) while((s32[]{:T(128)}, f32[1,256,2048]{2,1,0:T(8,128)}, ...), condition=%wide.region_7.8_spmd, body=%wide.region_4.7_spmd.sunk | while | flops 4298113024 | bytes 70254888 | solution.py:107
  138.2 1.3 collective-permute-start.1
  139.5 32.5 %collective-permute-done.1 = bf16[256,2048]{1,0:T(8,128)(2,1)} collective-permute-done((bf16[256,2048]{1,0:T(8,128)(2,1)S(1)}, bf16[256,2048]{1,0:T(8,128)(2,1)}, u32[]{:S(2)}, u32[]{:S(2)}) %collective-permute-start.1) | collective-permute-done | bytes 1048608 | tf_op jit(solution)/shard_map/while/body/eval_jaxpr/ppermute | solution.py:22
  172.0 1.3 collective-permute-start.1
  173.3 22.9 %collective-permute-done.1 = bf16[256,2048]{1,0:T(8,128)(2,1)} collective-permute-done((bf16[256,2048]{1,0:T(8,128)(2,1)S(1)}, bf16[256,2048]{1,0:T(8,128)(2,1)}, u32[]{:S(2)}, u32[]{:S(2)}) %collective-permute-start.1) | collective-permute-done | bytes 1048608 | tf_op jit(solution)/shard_map/while/body/eval_jaxpr/ppermute | solution.py:22
  196.2 1.3 collective-permute-start.1
  197.5 31.3 %collective-permute-done.1 = bf16[256,2048]{1,0:T(8,128)(2,1)} collective-permute-done((bf16[256,2048]{1,0:T(8,128)(2,1)S(1)}, bf16[256,2048]{1,0:T(8,128)(2,1)}, u32[]{:S(2)}, u32[]{:S(2)}) %collective-permute-start.1) | collective-permute-done | bytes 1048608 | tf_op jit(solution)/shard_map/while/body/eval_jaxpr/ppermute | solution.py:22
  228.8 1.3 collective-permute-start.1
  230.1 44.1 %collective-permute-done.1 = bf16[256,2048]{1,0:T(8,128)(2,1)} collective-permute-done((bf16[256,2048]{1,0:T(8,128)(2,1)S(1)}, bf16[256,2048]{1,0:T(8,128)(2,1)}, u32[]{:S(2)}, u32[]{:S(2)}) %collective-permute-start.1) | collective-permute-done | bytes 1048608 | tf_op jit(solution)/shard_map/while/body/eval_jaxpr/ppermute | solution.py:22
  274.2 8.5 %conditional.5 = ((bf16[256,2048]{1,0:T(8,128)(2,1)S(1)}, f32[1,256,2048]{2,1,0:T(8,128)})) conditional(s32[]{:T(128)} %convert_element_type.99, (bf16[256,2048]{1,0:T(8,128)(2,1)S(1)}, f32[1,256,2048]{2,1,0:T(8,128)}) %tuple.108, (bf16[1,256,2048]{2,1,0:T(8,128)(2,1)S(1)}, bf16[256,2048]{1,0:T(8,128)(2,1)}, bf16[2048,2048]{1,0:T(8,128)(2,1)}, ...), branch_computations={%region_5.5_spmd, %region_6.6_spmd} | conditional | flops 4298113024 | bytes 66060368 | solution.py:99
  274.2 6.2 %fusion.2 = f32[256,2048]{1,0:T(8,128)S(1)} fusion(bf16[2048,2048]{1,0:T(8,128)(2,1)} %get-tuple-element.350, bf16[256,2048]{1,0:T(8,128)(2,1)} %get-tuple-element.349, bf16[1,256,2048]{2,1,0:T(8,128)(2,1)S(1)} %get-tuple-element.348), kind=kOutput, calls=%fused_computation.7 | convolution fusion | flops 2149580800 | bytes 12582912 | tf_op jit(solution)/shard_map/while/body/eval_jaxpr/cond/branch_1_fun/dot_general | solution.py:90
  280.4 2.3 convolution_convert_fusion.1
  282.8 3.1 fusion.11
  286.0 33.3 %all-reduce.2.cloned.1.call-done = bf16[256,300]{1,0:T(8,128)(2,1)} async-done(((bf16[256,300]{1,0:T(8,128)(2,1)}), bf16[256,300]{1,0:T(8,128)(2,1)}) %all-reduce.2.cloned.1.call-update) | async-done | bytes 153616 | tf_op jit(solution)/shard_map/psum | solution.py:109
  319.3 2.6 convolution_subtract_fusion.1
  321.9 1.5 copy.8
  323.4 0.7 gather_fusion
  324.2 1.4 collective-permute-start.2
  325.6 2.6 collective-permute-done.2
  328.2 0.2 collective-permute-start.3
  328.4 5.0 %collective-permute-done.3 = bf16[128,256]{1,0:T(8,128)(2,1)S(1)} collective-permute-done((bf16[128,256]{1,0:T(8,128)(2,1)S(1)}, bf16[128,256]{1,0:T(8,128)(2,1)S(1)}, u32[]{:S(2)}, u32[]{:S(2)}) %collective-permute-start.3) | collective-permute-done | bytes 65568 | tf_op jit(solution)/shard_map/ppermute | solution.py:12
  333.4 0.4 collective-permute-start.4
  333.8 0.6 constant_dynamic-update-slice_fusion.16
  334.4 1.9 collective-permute-done.4
  336.3 2.5 collective-permute-start.5
  338.8 0.6 constant_dynamic-update-slice_fusion.3
  339.4 0.6 constant_dynamic-update-slice_fusion.2
  340.0 0.7 constant_dynamic-update-slice_fusion.1
  340.7 4.8 %collective-permute-done.5 = bf16[512,256]{1,0:T(8,128)(2,1)S(1)} collective-permute-done((bf16[512,256]{1,0:T(8,128)(2,1)S(1)}, bf16[512,256]{1,0:T(8,128)(2,1)S(1)}, u32[]{:S(2)}, u32[]{:S(2)}) %collective-permute-start.5) | collective-permute-done | bytes 262176 | tf_op jit(solution)/shard_map/ppermute | solution.py:12
  345.5 0.7 constant_dynamic-update-slice_fusion
  346.2 0.3 collective-permute-start.6
  346.5 13.6 %collective-permute-done.6 = bf16[1024,256]{1,0:T(8,128)(2,1)S(1)} collective-permute-done((bf16[1024,256]{1,0:T(8,128)(2,1)S(1)}, bf16[1024,256]{1,0:T(8,128)(2,1)S(1)}, u32[]{:S(2)}, u32[]{:S(2)}) %collective-permute-start.6) | collective-permute-done | bytes 524320 | tf_op jit(solution)/shard_map/ppermute | solution.py:12
  360.1 0.8 constant_dynamic-update-slice_fusion.11
  360.9 0.6 constant_dynamic-update-slice_fusion.10
  361.6 0.6 constant_dynamic-update-slice_fusion.9
  362.2 0.6 constant_dynamic-update-slice_fusion.8
  362.8 0.7 constant_dynamic-update-slice_fusion.7
  363.4 0.7 constant_dynamic-update-slice_fusion.6
  364.2 0.8 constant_dynamic-update-slice_fusion.5
  365.0 1.3 constant_dynamic-slice_fusion
  366.3 0.3 convolution_bitcast_fusion.1
  366.6 3.8 fusion.6
  (43 shorter events, 0.8 us)
Async XLA Ops:
  7.2 275.6 %copy-start = (bf16[1,300,2048]{2,1,0:T(8,128)(2,1)S(1)}, bf16[1,300,2048]{2,1,0:T(8,128)(2,1)}, u32[]{:S(2)}) copy-start(bf16[1,300,2048]{2,1,0:T(8,128)(2,1)} %param.15) | copy-start | bytes 3686404
  7.2 312.1 %all-reduce.2.cloned.1.call-start = ((), (), s32[]{:S(2)}) async-start(), calls=%async_computation | async-start | bytes 393216 | tf_op jit(solution)/shard_map/psum | solution.py:109
  10.1 27.4 %collective-permute-start = (bf16[256,2048]{1,0:T(8,128)(2,1)S(1)}, bf16[256,2048]{1,0:T(8,128)(2,1)S(1)}, u32[]{:S(2)}, u32[]{:S(2)}) collective-permute-start(bf16[256,2048]{1,0:T(8,128)(2,1)S(1)} %copy.23), channel_id=1, source_target_pairs={{0,1},{1,2},{2,3},{4,5},{5,6},{6,7},{8,9},{9,10},{10,11},{12,13},{... | collective-permute-start | bytes 3145736 | tf_op jit(solution)/shard_map/while/body/eval_jaxpr/ppermute | solution.py:22
  48.4 1.0 copy-start.1
  49.4 23.1 %collective-permute-start = (bf16[256,2048]{1,0:T(8,128)(2,1)S(1)}, bf16[256,2048]{1,0:T(8,128)(2,1)S(1)}, u32[]{:S(2)}, u32[]{:S(2)}) collective-permute-start(bf16[256,2048]{1,0:T(8,128)(2,1)S(1)} %copy.23), channel_id=1, source_target_pairs={{0,1},{1,2},{2,3},{4,5},{5,6},{6,7},{8,9},{9,10},{10,11},{12,13},{... | collective-permute-start | bytes 3145736 | tf_op jit(solution)/shard_map/while/body/eval_jaxpr/ppermute | solution.py:22
  72.6 1.0 copy-start.1
  73.6 36.3 %collective-permute-start = (bf16[256,2048]{1,0:T(8,128)(2,1)S(1)}, bf16[256,2048]{1,0:T(8,128)(2,1)S(1)}, u32[]{:S(2)}, u32[]{:S(2)}) collective-permute-start(bf16[256,2048]{1,0:T(8,128)(2,1)S(1)} %copy.23), channel_id=1, source_target_pairs={{0,1},{1,2},{2,3},{4,5},{5,6},{6,7},{8,9},{9,10},{10,11},{12,13},{... | collective-permute-start | bytes 3145736 | tf_op jit(solution)/shard_map/while/body/eval_jaxpr/ppermute | solution.py:22
  109.9 1.0 copy-start.1
  111.0 24.5 %collective-permute-start = (bf16[256,2048]{1,0:T(8,128)(2,1)S(1)}, bf16[256,2048]{1,0:T(8,128)(2,1)S(1)}, u32[]{:S(2)}, u32[]{:S(2)}) collective-permute-start(bf16[256,2048]{1,0:T(8,128)(2,1)S(1)} %copy.23), channel_id=1, source_target_pairs={{0,1},{1,2},{2,3},{4,5},{5,6},{6,7},{8,9},{9,10},{10,11},{12,13},{... | collective-permute-start | bytes 3145736 | tf_op jit(solution)/shard_map/while/body/eval_jaxpr/ppermute | solution.py:22
  135.5 1.0 copy-start.1
  136.5 1.7 copy-start.2
  138.2 33.8 %collective-permute-start.1 = (bf16[256,2048]{1,0:T(8,128)(2,1)S(1)}, bf16[256,2048]{1,0:T(8,128)(2,1)}, u32[]{:S(2)}, u32[]{:S(2)}) collective-permute-start(bf16[256,2048]{1,0:T(8,128)(2,1)S(1)} %get-tuple-element.536), channel_id=1, source_target_pairs={{1,0},{2,1},{3,2},{5,4},{6,5},{7,6},{9,8},{10,9},{11,10},{13,12},{... | collective-permute-start | bytes 3145736 | tf_op jit(solution)/shard_map/while/body/eval_jaxpr/ppermute | solution.py:22
  172.0 24.2 %collective-permute-start.1 = (bf16[256,2048]{1,0:T(8,128)(2,1)S(1)}, bf16[256,2048]{1,0:T(8,128)(2,1)}, u32[]{:S(2)}, u32[]{:S(2)}) collective-permute-start(bf16[256,2048]{1,0:T(8,128)(2,1)S(1)} %get-tuple-element.536), channel_id=1, source_target_pairs={{1,0},{2,1},{3,2},{5,4},{6,5},{7,6},{9,8},{10,9},{11,10},{13,12},{... | collective-permute-start | bytes 3145736 | tf_op jit(solution)/shard_map/while/body/eval_jaxpr/ppermute | solution.py:22
  196.2 32.6 %collective-permute-start.1 = (bf16[256,2048]{1,0:T(8,128)(2,1)S(1)}, bf16[256,2048]{1,0:T(8,128)(2,1)}, u32[]{:S(2)}, u32[]{:S(2)}) collective-permute-start(bf16[256,2048]{1,0:T(8,128)(2,1)S(1)} %get-tuple-element.536), channel_id=1, source_target_pairs={{1,0},{2,1},{3,2},{5,4},{6,5},{7,6},{9,8},{10,9},{11,10},{13,12},{... | collective-permute-start | bytes 3145736 | tf_op jit(solution)/shard_map/while/body/eval_jaxpr/ppermute | solution.py:22
  228.8 45.4 %collective-permute-start.1 = (bf16[256,2048]{1,0:T(8,128)(2,1)S(1)}, bf16[256,2048]{1,0:T(8,128)(2,1)}, u32[]{:S(2)}, u32[]{:S(2)}) collective-permute-start(bf16[256,2048]{1,0:T(8,128)(2,1)S(1)} %get-tuple-element.536), channel_id=1, source_target_pairs={{1,0},{2,1},{3,2},{5,4},{6,5},{7,6},{9,8},{10,9},{11,10},{13,12},{... | collective-permute-start | bytes 3145736 | tf_op jit(solution)/shard_map/while/body/eval_jaxpr/ppermute | solution.py:22
  274.2 6.2 %copy-start.7 = (bf16[2048,2048]{1,0:T(8,128)(2,1)S(1)}, bf16[2048,2048]{1,0:T(8,128)(2,1)}, u32[]{:S(2)}) copy-start(bf16[2048,2048]{1,0:T(8,128)(2,1)} %get-tuple-element.351) | copy-start | bytes 25165828 | tf_op jit(solution)/shard_map/while/body/eval_jaxpr/cond
  280.4 2.4 copy-start.3
  282.8 3.2 copy-start.6
  282.8 36.5 %copy-start.4 = (f32[1,256,2048]{2,1,0:T(8,128)S(1)}, f32[1,256,2048]{2,1,0:T(8,128)}, u32[]{:S(2)}) copy-start(f32[1,256,2048]{2,1,0:T(8,128)} %get-tuple-element.367) | copy-start | bytes 6291460
  323.4 23.1 %copy-start.5 = (s32[8,256]{1,0:T(8,128)S(1)}, s32[8,256]{1,0:T(8,128)}, u32[]{:S(2)}) copy-start(s32[8,256]{1,0:T(8,128)} %param.17) | copy-start | bytes 24580
  324.2 4.0 %collective-permute-start.2 = (bf16[64,256]{1,0:T(8,128)(2,1)S(1)}, bf16[64,256]{1,0:T(8,128)(2,1)S(1)}, u32[]{:S(2)}, u32[]{:S(2)}) collective-permute-start(bf16[64,256]{1,0:T(8,128)(2,1)S(1)} %get-tuple-element.397), channel_id=1, source_target_pairs={{0,31},{1,0},{2,1},{3,2},{4,3},{5,4},{6,5},{7,6},{8,7},{9,8},{10,9... | collective-permute-start | bytes 98312 | tf_op jit(solution)/shard_map/ppermute | solution.py:12
  328.2 5.2 %collective-permute-start.3 = (bf16[128,256]{1,0:T(8,128)(2,1)S(1)}, bf16[128,256]{1,0:T(8,128)(2,1)S(1)}, u32[]{:S(2)}, u32[]{:S(2)}) collective-permute-start(bf16[128,256]{1,0:T(8,128)(2,1)S(1)} %pad_maximum_fusion.2), channel_id=1, source_target_pairs={{0,30},{1,31},{2,0},{3,1},{4,2},{5,3},{6,4},{7,5},{8,6},{9,7},{10,... | collective-permute-start | bytes 196616 | tf_op jit(solution)/shard_map/ppermute | solution.py:12
  333.4 2.9 collective-permute-start.4
  336.3 9.2 %collective-permute-start.5 = (bf16[512,256]{1,0:T(8,128)(2,1)S(1)}, bf16[512,256]{1,0:T(8,128)(2,1)S(1)}, u32[]{:S(2)}, u32[]{:S(2)}) collective-permute-start(bf16[512,256]{1,0:T(8,128)(2,1)S(1)} %pad_maximum_fusion), channel_id=1, source_target_pairs={{0,24},{1,25},{2,26},{3,27},{4,28},{5,29},{6,30},{7,31},{8,0},{9,1... | collective-permute-start | bytes 786440 | tf_op jit(solution)/shard_map/ppermute | solution.py:12
  346.2 13.9 %collective-permute-start.6 = (bf16[1024,256]{1,0:T(8,128)(2,1)S(1)}, bf16[1024,256]{1,0:T(8,128)(2,1)S(1)}, u32[]{:S(2)}, u32[]{:S(2)}) collective-permute-start(bf16[1024,256]{1,0:T(8,128)(2,1)S(1)} %get-tuple-element.398), channel_id=1, source_target_pairs={{0,16},{1,17},{2,18},{3,19},{4,20},{5,21},{6,22},{7,23},{8,24},{9,... | collective-permute-start | bytes 1572872 | tf_op jit(solution)/shard_map/ppermute | solution.py:12
Sparse Core Ops, SparseCore 0:
  286.1 33.1 all-reduce.1
